TPU v7x, 256 devices: a whole 4x4x8 slice. The times are simulated.
256 devices in a mesh: group: 16 (over z_lo, y), tok: 16 (over z_hi, x, core).
Axes of the slice: x: 4, y: 4, z: 8 (z_hi: 2, z_lo: 4; z = z_hi * 4 + z_lo), core: 2. Of those that a mesh axis runs over, the one named last changes fastest.
Arguments:
- tokens: bfloat16 [131072, 2048], P(('group', 'tok')), may hold values from -94 to 94
- learning_rates: float32 [2, 131072], P(None, 'group'), may hold values from 0.1 to 1
- channel_gains: float32 [2, 5, 2048], P(None, None, 'tok'), may hold values from 0.3 to 3
- fast_init: float32 [2, 3, 16, 128, 128], P(None, None, 'tok'), may hold values from -0.5 to 0.5
- step_size: float32 [2, 16], P(None, 'tok'), may hold values from 0.05 to 1
- update_table: int32 [2, 16], replicated, may hold values 0 or 1
Outputs:
- mixed: bfloat16 [131072, 2048], P(('group', 'tok'))
All inputs are finite; a program needn't handle non-finite values.
Results may differ from a plain program's by a relative error of at most 0.033.
Values may be sent and summed in bfloat16 or wider, within the bound.
No kernel may reach another device: no remote copies, remote signals or barrier semaphores. Data moves between devices by JAX's collectives and lax.ppermute only.
A program may use at most 64 MiB of HBM per device.

v0:
```python
import jax
import jax.numpy as jnp
from jax import lax
from jax.sharding import PartitionSpec as P

NS_STEPS = 5
MUON_A = 3.4445
MUON_B = -4.775
MUON_C = 2.0315
EPSILON = 1e-06


def passed_along(value, axis, by):
    size = lax.axis_size(axis)
    pairs = [(i, i + by) for i in range(size) if 0 <= i + by < size]
    return lax.ppermute(value, axis, pairs)


def orthogonalize(gradient):
    scaling = lax.rsqrt(jnp.sum(gradient * gradient, axis=(-2, -1), keepdims=True) + EPSILON)
    current = gradient * scaling
    for repeat in range(NS_STEPS):
        square = jnp.einsum("...ij,...kj->...ik", current, current, precision=lax.Precision.HIGHEST)
        polynom = MUON_B * square + MUON_C * jnp.einsum(
            "...ij,...jk->...ik", square, square, precision=lax.Precision.HIGHEST
        )
        current = MUON_A * current + jnp.einsum(
            "...ij,...jk->...ik", polynom, current, precision=lax.Precision.HIGHEST
        )
    return current


def layer_group(stream, entering, gain_rows, rates_row, steps_row, update_flag, inverse):
    row_count, channel_count = stream.shape
    heads_n = entering.shape[1]
    head_dim = entering.shape[2]
    normed = stream.astype(jnp.float32) * inverse[:, None] * gain_rows[0]
    queries = (normed * gain_rows[1]).astype(jnp.bfloat16).reshape(row_count, heads_n, head_dim)
    keys_in = (normed * gain_rows[2]).astype(jnp.bfloat16).reshape(row_count, heads_n, head_dim)
    values_in = (normed * gain_rows[3]).astype(jnp.bfloat16).reshape(row_count, heads_n, head_dim)
    rounded = entering.astype(jnp.bfloat16)
    gate_q = jnp.einsum("thi,hij->thj", queries, rounded[0], preferred_element_type=jnp.float32)
    up_q = jnp.einsum("thi,hij->thj", queries, rounded[1], preferred_element_type=jnp.float32)
    hidden_q = (jax.nn.silu(gate_q) * up_q).astype(jnp.bfloat16)
    output = jnp.einsum(
        "thj,hjk->thk", hidden_q, rounded[2], preferred_element_type=jnp.float32
    ).reshape(row_count, channel_count)
    mixed_rows = (stream.astype(jnp.float32) + gain_rows[4] * output).astype(jnp.bfloat16)
    gate_k = jnp.einsum("thi,hij->thj", keys_in, rounded[0], preferred_element_type=jnp.float32)
    up_k = jnp.einsum("thi,hij->thj", keys_in, rounded[1], preferred_element_type=jnp.float32)
    sigmoid_k = jax.nn.sigmoid(gate_k)
    active_k = gate_k * sigmoid_k
    hidden_k = (active_k * up_k).astype(jnp.bfloat16)
    targets = (rates_row[:, None, None] * values_in.astype(jnp.float32)).astype(jnp.bfloat16)
    back_hidden = jnp.einsum(
        "thk,hjk->thj", targets, rounded[2], preferred_element_type=jnp.float32
    )
    back_up = (back_hidden * active_k).astype(jnp.bfloat16)
    back_gate = (back_hidden * up_k * sigmoid_k * (1.0 + gate_k * (1.0 - sigmoid_k))).astype(
        jnp.bfloat16
    )
    grad_gate = jnp.einsum("thi,thj->hij", keys_in, back_gate, preferred_element_type=jnp.float32)
    grad_up = jnp.einsum("thi,thj->hij", keys_in, back_up, preferred_element_type=jnp.float32)
    grad_down = jnp.einsum("thj,thk->hjk", hidden_k, targets, preferred_element_type=jnp.float32)
    direction = orthogonalize(jnp.stack([grad_gate, grad_up, grad_down]))
    moved_state = entering + (update_flag * steps_row)[None, :, None, None] * direction
    norm_before = jnp.sqrt(jnp.sum(entering * entering, axis=2, keepdims=True) + EPSILON)
    norm_after = jnp.sqrt(jnp.sum(moved_state * moved_state, axis=2, keepdims=True) + EPSILON)
    return (mixed_rows, moved_state * (norm_before / norm_after))


def pass_on(outgoing):
    return passed_along(outgoing, "group", 1)


def body(tokens, learning_rates, channel_gains, fast_init, step_size, update_table):
    start_stream = lax.all_to_all(tokens, "tok", split_axis=1, concat_axis=0, tiled=True)
    group_count = lax.axis_size("group")
    group_index = lax.axis_index("group")
    width_all = start_stream.shape[1] * lax.axis_size("tok")
    layer_count = fast_init.shape[0]
    zero_state = jnp.zeros(fast_init.shape[1:], jnp.float32)

    def tick_work(stream, outgoing, layer_now, active, inverse):
        received = pass_on(outgoing)
        initial = lax.dynamic_index_in_dim(fast_init, layer_now, 0, keepdims=False)
        entering = jnp.where(group_index == 0, initial, received)
        gain_rows = lax.dynamic_index_in_dim(channel_gains, layer_now, 0, keepdims=False)
        rates_row = lax.dynamic_index_in_dim(learning_rates, layer_now, 0, keepdims=False)
        steps_row = lax.dynamic_index_in_dim(step_size, layer_now, 0, keepdims=False)
        table_cell = lax.dynamic_slice(
            update_table, (jnp.asarray(layer_now, jnp.int32), group_index), (1, 1)
        )
        update_flag = table_cell[0, 0].astype(jnp.float32)

        def working(operands):
            return layer_group(
                operands[0], operands[1], gain_rows, rates_row, steps_row, update_flag, inverse
            )

        def resting(operands):
            return (operands[0], operands[2])

        return lax.cond(active, working, resting, (stream, entering, outgoing))

    final_stream = start_stream
    for layer_now in range(layer_count):
        widened = final_stream.astype(jnp.float32)
        totals = lax.psum(jnp.sum(widened * widened, axis=1), "tok")
        inverse = lax.rsqrt(totals / width_all + EPSILON)

        def one_tick(tick_index, loop_state):
            stream, outgoing = loop_state
            active = tick_index == group_index
            return tick_work(stream, outgoing, layer_now, active, inverse)

        final_stream, last_state = lax.fori_loop(
            0, group_count, one_tick, (final_stream, zero_state)
        )
    return lax.all_to_all(final_stream, "tok", split_axis=0, concat_axis=1, tiled=True)


def solution(mesh):
    in_specs = (
        P(("group", "tok"), None),
        P(None, "group"),
        P(None, None, "tok"),
        P(None, None, "tok", None, None),
        P(None, "tok"),
        P(),
    )
    out_specs = P(("group", "tok"), None)
    return jax.shard_map(body, mesh=mesh, in_specs=in_specs, out_specs=out_specs, check_vma=False)
```

profile of v0, /device:TPU:120, one launch (start us, length us, event | category | flops | bytes accessed | tf_op | source)
XLA Modules:
  0.0 1390.3 jit_solution(5411178419686325323)
XLA Ops:
  3.5 8.5 all-to-all-start
  14.0 35.7 %all-to-all-done = bf16[512,16,128]{2,0,1:T(8,128)(2,1)} async-done(((bf16[512,16,128]{2,0,1:T(8,128)(2,1)}), bf16[512,16,128]{2,0,1:T(8,128)(2,1)}, u32[]{:S(2)}, u32[]{:S(2)}) %all-to-all-start) | async-done | bytes 2097184 | tf_op jit(solution)/shard_map/all_to_all | solution.py:77
  52.5 87.6 %psum.14 = f32[8192]{0:T(1024)S(1)} all-reduce(f32[8192]{0:T(1024)S(1)} %bitcast.261), channel_id=1, replica_groups=mesh['group'=16,'tok'=16] {'tok'}, use_global_device_ids=true, to_apply=%region_1.0 | all-reduce | flops 8192 | bytes 65536 | tf_op jit(solution)/shard_map/psum | solution.py:109
  140.2 663.9 %while.34 = (s32[]{:T(128)}, bf16[8192,128]{1,0:T(8,128)(2,1)}, f32[3,1,128,128]{3,2,0,1:T(8,128)S(1)}, s32[]{:T(128)}, f32[2,5,128]{2,1,0:T(8,128)S(1)}, /*inde...) while((s32[]{:T(128)}, bf16[8192,128]{1,0:T(8,128)(2,1)}, ...), condition=%wide.region_8.9_spmd, body=%wide.region_2.8_spmd.sunk | while | flops 3632480256 | bytes 94034832 | solution.py:117
  164.1 24.6 %collective-permute-done = f32[3,1,128,128]{3,2,0,1:T(8,128)S(1)} collective-permute-done((f32[3,1,128,128]{3,2,0,1:T(8,128)S(1)}, f32[3,1,128,128]{3,2,0,1:T(8,128)S(1)}, u32[]{:S(2)}, u32[]{:S(2)}) %collective-permute-start) | collective-permute-done | bytes 196640 | tf_op jit(solution)/shard_map/while/body/eval_jaxpr/ppermute | solution.py:16
  190.0 7.5 collective-permute-done
  198.8 8.1 collective-permute-done
  208.2 8.4 collective-permute-done
  217.9 8.4 collective-permute-done
  227.5 9.8 collective-permute-done
  238.7 10.8 collective-permute-done
  250.8 9.7 collective-permute-done
  261.8 9.0 collective-permute-done
  272.1 7.4 collective-permute-done
  280.8 7.6 collective-permute-done
  289.7 8.4 collective-permute-done
  299.4 469.8 %collective-permute-done = f32[3,1,128,128]{3,2,0,1:T(8,128)S(1)} collective-permute-done((f32[3,1,128,128]{3,2,0,1:T(8,128)S(1)}, f32[3,1,128,128]{3,2,0,1:T(8,128)S(1)}, u32[]{:S(2)}, u32[]{:S(2)}) %collective-permute-start) | collective-permute-done | bytes 196640 | tf_op jit(solution)/shard_map/while/body/eval_jaxpr/ppermute | solution.py:16
  769.2 34.9 %conditional.4 = ((bf16[8192,128]{1,0:T(8,128)(2,1)}, f32[3,1,128,128]{3,2,0,1:T(8,128)S(1)})) conditional(s32[]{:T(128)} %convert_element_type.267, (bf16[8192,128]{1,0:T(8,128)(2,1)}, f32[3,1,128,128]{3,2,0,1:T(8,128)S(1)}) %tuple.101, (bf16[8192,128]{1,0:T(8,128)(2,1)}, f32[2,5,128]{2,1,0:T(8,128)S(1)}, pred[]{:T(512)}, ...), branch_computations={%region_3.3_spmd, %region_4.7_spmd} | conditional | flops 3632480256 | bytes 93248136 | solution.py:104
  790.4 7.2 fusion.3
  806.8 84.2 %psum.15 = f32[8192]{0:T(1024)S(1)} all-reduce(f32[8192]{0:T(1024)S(1)} %multiply_reduce_fusion.4), channel_id=1, replica_groups=mesh['group'=16,'tok'=16] {'tok'}, use_global_device_ids=true, to_apply=%region_10.11 | all-reduce | flops 8192 | bytes 65536 | tf_op jit(solution)/shard_map/psum | solution.py:109
  891.0 453.8 %while.35 = (s32[]{:T(128)}, bf16[8192,128]{1,0:T(8,128)(2,1)}, f32[3,1,128,128]{3,2,0,1:T(8,128)S(1)}, s32[]{:T(128)}, f32[2,5,128]{2,1,0:T(8,128)S(1)}, /*inde...) while((s32[]{:T(128)}, bf16[8192,128]{1,0:T(8,128)(2,1)}, ...), condition=%wide.region_17.18_spmd, body=%wide.region_11.17_spmd.sunk | while | flops 3632480256 | bytes 94034832 | solution.py:117
  929.3 7.8 collective-permute-done.1
  938.4 7.8 collective-permute-done.1
  978.4 7.3 collective-permute-done.1
  987.0 9.8 collective-permute-done.1
  998.0 8.6 collective-permute-done.1
  1008.0 7.4 collective-permute-done.1
  1016.7 7.8 collective-permute-done.1
  1025.8 8.4 collective-permute-done.1
  1035.4 273.3 %collective-permute-done.1 = f32[3,1,128,128]{3,2,0,1:T(8,128)S(1)} collective-permute-done((f32[3,1,128,128]{3,2,0,1:T(8,128)S(1)}, f32[3,1,128,128]{3,2,0,1:T(8,128)S(1)}, u32[]{:S(2)}, u32[]{:S(2)}) %collective-permute-start.1) | collective-permute-done | bytes 196640 | tf_op jit(solution)/shard_map/while/body/eval_jaxpr/ppermute | solution.py:16
  1308.7 36.1 %conditional.5 = ((bf16[8192,128]{1,0:T(8,128)(2,1)}, f32[3,1,128,128]{3,2,0,1:T(8,128)S(1)})) conditional(s32[]{:T(128)} %convert_element_type.268, (bf16[8192,128]{1,0:T(8,128)(2,1)}, f32[3,1,128,128]{3,2,0,1:T(8,128)S(1)}) %tuple.104, (bf16[8192,128]{1,0:T(8,128)(2,1)}, f32[2,5,128]{2,1,0:T(8,128)S(1)}, pred[]{:T(512)}, ...), branch_computations={%region_12.12_spmd, %region_13.16_spmd} | conditional | flops 3632480256 | bytes 93248136 | solution.py:104
  1344.8 37.3 %all_to_all.38 = bf16[16,512,128]{2,1,0:T(8,128)(2,1)} all-to-all(bf16[16,512,128]{2,1,0:T(8,128)(2,1)} %bitcast.82), channel_id=1, replica_groups=mesh['group'=16,'tok'=16] {'tok'}, dimensions={0} | all-to-all | bytes 4194304 | tf_op jit(solution)/shard_map/all_to_all | solution.py:120
  (164 shorter events, 185.0 us)
Async XLA Ops:
  3.5 46.3 %all-to-all-start = ((bf16[512,16,128]{2,0,1:T(8,128)(2,1)}), bf16[512,16,128]{2,0,1:T(8,128)(2,1)}, u32[]{:S(2)}, u32[]{:S(2)}) async-start(bf16[512,16,128]{2,0,1:T(8,128)(2,1)} %copy_bitcast_fusion), calls=%async_computation | async-start | bytes 4194304 | tf_op jit(solution)/shard_map/all_to_all | solution.py:77
  140.2 7.6 collective-permute-start
  147.7 7.6 collective-permute-start
  155.3 7.6 collective-permute-start
  162.8 25.9 %collective-permute-start = (f32[3,1,128,128]{3,2,0,1:T(8,128)S(1)}, f32[3,1,128,128]{3,2,0,1:T(8,128)S(1)}, u32[]{:S(2)}, u32[]{:S(2)}) collective-permute-start(f32[3,1,128,128]{3,2,0,1:T(8,128)S(1)} %get-tuple-element.889), channel_id=1, source_target_pairs={{0,16},{16,32},{32,48},{48,64},{64,80},{80,96},{96,112},{112,128},... | collective-permute-start | bytes 589832 | tf_op jit(solution)/shard_map/while/body/eval_jaxpr/ppermute | solution.py:16
  188.7 8.8 collective-permute-start
  197.5 9.4 collective-permute-start
  206.9 9.7 collective-permute-start
  216.6 9.7 collective-permute-start
  226.3 11.1 collective-permute-start
  237.4 12.1 collective-permute-start
  249.5 11.0 collective-permute-start
  260.5 10.3 collective-permute-start
  270.8 8.7 collective-permute-start
  279.5 8.9 collective-permute-start
  288.4 9.7 collective-permute-start
  298.1 471.1 %collective-permute-start = (f32[3,1,128,128]{3,2,0,1:T(8,128)S(1)}, f32[3,1,128,128]{3,2,0,1:T(8,128)S(1)}, u32[]{:S(2)}, u32[]{:S(2)}) collective-permute-start(f32[3,1,128,128]{3,2,0,1:T(8,128)S(1)} %get-tuple-element.889), channel_id=1, source_target_pairs={{0,16},{16,32},{32,48},{48,64},{64,80},{80,96},{96,112},{112,128},... | collective-permute-start | bytes 589832 | tf_op jit(solution)/shard_map/while/body/eval_jaxpr/ppermute | solution.py:16
  905.0 7.6 collective-permute-start.1
  912.6 7.6 collective-permute-start.1
  920.1 7.9 collective-permute-start.1
  928.0 9.1 collective-permute-start.1
  937.1 9.1 collective-permute-start.1
  946.2 8.2 collective-permute-start.1
  954.5 7.6 collective-permute-start.1
  962.0 7.6 collective-permute-start.1
  977.1 8.6 collective-permute-start.1
  985.7 11.1 collective-permute-start.1
  996.8 9.9 collective-permute-start.1
  1006.7 8.7 collective-permute-start.1
  1015.4 9.1 collective-permute-start.1
  1024.5 9.7 collective-permute-start.1
  1034.1 274.6 %collective-permute-start.1 = (f32[3,1,128,128]{3,2,0,1:T(8,128)S(1)}, f32[3,1,128,128]{3,2,0,1:T(8,128)S(1)}, u32[]{:S(2)}, u32[]{:S(2)}) collective-permute-start(f32[3,1,128,128]{3,2,0,1:T(8,128)S(1)} %get-tuple-element.925), channel_id=1, source_target_pairs={{0,16},{16,32},{32,48},{48,64},{64,80},{80,96},{96,112},{112,128},... | collective-permute-start | bytes 589832 | tf_op jit(solution)/shard_map/while/body/eval_jaxpr/ppermute | solution.py:16
  (9 other events, 471.6 us)
where the time goes:
time: 1410 us; the launch traced here: 1390 us
  waiting for transfers between devices  1030 us (73%)
  blocking collectives  209 us (15%)
  matrix products  65.7 us (5%)
  starting transfers between devices  49.5 us (4%)
  local copies, waits for them, and re-layouts  15.9 us (1%)
  loops' own time  15.5 us (1%)
    ppermute x32, waiting for transfers between devices, passed_along(): return lax.ppermute(value, axis, pairs)  991 us
    psum x2, blocking collectives, body(): totals = lax.psum(jnp.sum(widened * widened, axis=1), 'tok')  172 us
    ppermute x32, starting transfers between devices, passed_along(): return lax.ppermute(value, axis, pairs)  41 us
    all_to_all x1, blocking collectives, body(): lax.all_to_all(final_stream, 'tok', split_axis=0, concat_axis=1, tiled=True)  37.3 us
    all_to_all x1, waiting for transfers between devices, body(): lax.all_to_all(tokens, 'tok', split_axis=1, concat_axis=0, tiled=True)  35.7 us
  transfers between devices with their start and end apart: 33, of which 33 were waited for; matrix products, arithmetic and copies ran while one was open for 0% of the time, Pallas kernels for 0%

commit v1 on v0

--- a/solution.py
+++ b/solution.py
@@ -106,7 +106,7 @@
     final_stream = start_stream
     for layer_now in range(layer_count):
         widened = final_stream.astype(jnp.float32)
-        totals = lax.psum(jnp.sum(widened * widened, axis=1), "tok")
+        totals = jnp.sum(lax.all_gather(jnp.sum(widened * widened, axis=1), "tok"), axis=0)
         inverse = lax.rsqrt(totals / width_all + EPSILON)
 
         def one_tick(tick_index, loop_state):

time: 1410 us -> 1330 us (0.943)
  blocking collectives: 209 us -> 96.1 us
  waiting for transfers between devices: 1030 us -> 1060 us
  loops' own time: 15.5 us -> 29.9 us
    psum x2 -> x0, blocking collectives: 172 us -> none  [body(): totals = lax.psum(jnp.sum(widened * widened, axis=1), 'tok')]
    all_gather x0 -> x2, blocking collectives: none -> 60.1 us  [body(): lax.all_gather(jnp.sum(widened * widened, axis=1), 'tok')]
    ppermute x32, waiting for transfers between devices: 991 us -> 1020 us  [passed_along(): return lax.ppermute(value, axis, pairs)]
    another operation x2, loops' own time: 14.5 us -> 28.9 us  [body(): lax.fori_loop(0, group_count, one_tick, (final_stream, zero_state))]
where the time goes in v1:
time: 1330 us; the launch traced here: 1320 us
  waiting for transfers between devices  1060 us (80%)
  blocking collectives  96.1 us (7%)
  matrix products  65.7 us (5%)
  starting transfers between devices  49.5 us (4%)
  loops' own time  29.9 us (2%)
  local copies, waits for them, and re-layouts  18.7 us (1%)
    ppermute x32, waiting for transfers between devices, passed_along(): return lax.ppermute(value, axis, pairs)  1020 us
    all_gather x2, blocking collectives, body(): lax.all_gather(jnp.sum(widened * widened, axis=1), 'tok')  60.1 us
    ppermute x32, starting transfers between devices, passed_along(): return lax.ppermute(value, axis, pairs)  41 us
    all_to_all x1, blocking collectives, body(): lax.all_to_all(final_stream, 'tok', split_axis=0, concat_axis=1, tiled=True)  36.1 us
    all_to_all x1, waiting for transfers between devices, body(): lax.all_to_all(tokens, 'tok', split_axis=1, concat_axis=0, tiled=True)  35.7 us
    another operation x2, loops' own time, body(): lax.fori_loop(0, group_count, one_tick, (final_stream, zero_state))  28.9 us
  transfers between devices with their start and end apart: 33, of which 33 were waited for; matrix products, arithmetic and copies ran while one was open for 0% of the time, Pallas kernels for 0%

profile of v1, /device:TPU:120, one launch (start us, length us, event | category | flops | bytes accessed | tf_op | source)
XLA Modules:
  0.0 1323.4 jit_solution(7694147022761658496)
XLA Ops:
  3.5 8.5 all-to-all-start
  14.0 35.7 %all-to-all-done = bf16[512,16,128]{2,0,1:T(8,128)(2,1)} async-done(((bf16[512,16,128]{2,0,1:T(8,128)(2,1)}), bf16[512,16,128]{2,0,1:T(8,128)(2,1)}, u32[]{:S(2)}, u32[]{:S(2)}) %all-to-all-start) | async-done | bytes 2097184 | tf_op jit(solution)/shard_map/all_to_all | solution.py:77
  52.5 33.4 %all-gather.1 = f32[16,1,8192]{2,1,0:T(1,128)S(1)} all-gather(f32[1,1,8192]{2,1,0:T(1,128)S(1)} %reshape.603), channel_id=1, replica_groups=mesh['group'=16,'tok'=16] {'tok'}, dimensions={0}, use_global_device_ids=true | all-gather | bytes 557056 | tf_op jit(solution)/shard_map/all_gather | solution.py:109
  86.3 695.2 %while.34 = (s32[]{:T(128)}, bf16[8192,128]{1,0:T(8,128)(2,1)}, f32[3,1,128,128]{3,2,0,1:T(8,128)S(1)}, s32[]{:T(128)}, f32[2,5,128]{2,1,0:T(8,128)S(1)}, /*inde...) while((s32[]{:T(128)}, bf16[8192,128]{1,0:T(8,128)(2,1)}, ...), condition=%wide.region_8.9_spmd, body=%wide.region_2.8_spmd.sunk | while | flops 3632480256 | bytes 94034832 | solution.py:117
  102.1 7.7 collective-permute-done
  126.9 16.8 %collective-permute-done = f32[3,1,128,128]{3,2,0,1:T(8,128)S(1)} collective-permute-done((f32[3,1,128,128]{3,2,0,1:T(8,128)S(1)}, f32[3,1,128,128]{3,2,0,1:T(8,128)S(1)}, u32[]{:S(2)}, u32[]{:S(2)}) %collective-permute-start) | collective-permute-done | bytes 196640 | tf_op jit(solution)/shard_map/while/body/eval_jaxpr/ppermute | solution.py:16
  145.0 7.8 collective-permute-done
  154.1 8.1 collective-permute-done
  163.4 8.4 collective-permute-done
  173.1 8.9 collective-permute-done
  183.3 10.5 collective-permute-done
  195.1 10.6 collective-permute-done
  206.9 9.3 collective-permute-done
  226.4 7.8 collective-permute-done
  235.5 8.1 collective-permute-done
  244.9 8.4 collective-permute-done
  254.6 491.2 %collective-permute-done = f32[3,1,128,128]{3,2,0,1:T(8,128)S(1)} collective-permute-done((f32[3,1,128,128]{3,2,0,1:T(8,128)S(1)}, f32[3,1,128,128]{3,2,0,1:T(8,128)S(1)}, u32[]{:S(2)}, u32[]{:S(2)}) %collective-permute-start) | collective-permute-done | bytes 196640 | tf_op jit(solution)/shard_map/while/body/eval_jaxpr/ppermute | solution.py:16
  745.8 35.7 %conditional.4 = ((bf16[8192,128]{1,0:T(8,128)(2,1)}, f32[3,1,128,128]{3,2,0,1:T(8,128)S(1)})) conditional(s32[]{:T(128)} %convert_element_type.267, (bf16[8192,128]{1,0:T(8,128)(2,1)}, f32[3,1,128,128]{3,2,0,1:T(8,128)S(1)}) %tuple.103, (bf16[8192,128]{1,0:T(8,128)(2,1)}, f32[2,5,128]{2,1,0:T(8,128)S(1)}, pred[]{:T(512)}, ...), branch_computations={%region_3.3_spmd, %region_4.7_spmd} | conditional | flops 3632480256 | bytes 93248136 | solution.py:104
  784.2 26.7 %all-gather = f32[131072]{0:T(1024)} all-gather(f32[8192]{0:T(1024)S(1)} %multiply_reduce_fusion.4), channel_id=2, replica_groups=mesh['group'=16,'tok'=16] {'tok'}, dimensions={0}, use_global_device_ids=true | all-gather | bytes 557056 | tf_op jit(solution)/shard_map/all_gather | solution.py:109
  812.2 467.0 %while.35 = (s32[]{:T(128)}, bf16[8192,128]{1,0:T(8,128)(2,1)}, f32[3,1,128,128]{3,2,0,1:T(8,128)S(1)}, s32[]{:T(128)}, f32[2,5,128]{2,1,0:T(8,128)S(1)}, /*inde...) while((s32[]{:T(128)}, bf16[8192,128]{1,0:T(8,128)(2,1)}, ...), condition=%wide.region_17.18_spmd, body=%wide.region_11.17_spmd.sunk | while | flops 3632480256 | bytes 94034832 | solution.py:117
  827.6 7.7 collective-permute-done.1
  867.8 7.7 collective-permute-done.1
  876.8 7.9 collective-permute-done.1
  901.9 8.0 collective-permute-done.1
  911.2 9.3 collective-permute-done.1
  921.8 7.7 collective-permute-done.1
  930.8 7.7 collective-permute-done.1
  939.8 8.1 collective-permute-done.1
  949.2 8.4 collective-permute-done.1
  958.8 283.5 %collective-permute-done.1 = f32[3,1,128,128]{3,2,0,1:T(8,128)S(1)} collective-permute-done((f32[3,1,128,128]{3,2,0,1:T(8,128)S(1)}, f32[3,1,128,128]{3,2,0,1:T(8,128)S(1)}, u32[]{:S(2)}, u32[]{:S(2)}) %collective-permute-start.1) | collective-permute-done | bytes 196640 | tf_op jit(solution)/shard_map/while/body/eval_jaxpr/ppermute | solution.py:16
  1242.4 36.9 %conditional.5 = ((bf16[8192,128]{1,0:T(8,128)(2,1)}, f32[3,1,128,128]{3,2,0,1:T(8,128)S(1)})) conditional(s32[]{:T(128)} %convert_element_type.268, (bf16[8192,128]{1,0:T(8,128)(2,1)}, f32[3,1,128,128]{3,2,0,1:T(8,128)S(1)}) %tuple.106, (bf16[8192,128]{1,0:T(8,128)(2,1)}, f32[2,5,128]{2,1,0:T(8,128)S(1)}, pred[]{:T(512)}, ...), branch_computations={%region_12.12_spmd, %region_13.16_spmd} | conditional | flops 3632480256 | bytes 93248136 | solution.py:104
  1279.3 36.1 %all_to_all.38 = bf16[16,512,128]{2,1,0:T(8,128)(2,1)} all-to-all(bf16[16,512,128]{2,1,0:T(8,128)(2,1)} %bitcast.82), channel_id=1, replica_groups=mesh['group'=16,'tok'=16] {'tok'}, dimensions={0} | all-to-all | bytes 4194304 | tf_op jit(solution)/shard_map/all_to_all | solution.py:120
  (165 shorter events, 192.0 us)
Async XLA Ops:
  3.5 46.3 %all-to-all-start = ((bf16[512,16,128]{2,0,1:T(8,128)(2,1)}), bf16[512,16,128]{2,0,1:T(8,128)(2,1)}, u32[]{:S(2)}, u32[]{:S(2)}) async-start(bf16[512,16,128]{2,0,1:T(8,128)(2,1)} %copy_bitcast_fusion), calls=%async_computation | async-start | bytes 4194304 | tf_op jit(solution)/shard_map/all_to_all | solution.py:77
  100.8 9.0 collective-permute-start
  109.8 8.2 collective-permute-start
  118.0 7.6 collective-permute-start
  125.6 18.1 %collective-permute-start = (f32[3,1,128,128]{3,2,0,1:T(8,128)S(1)}, f32[3,1,128,128]{3,2,0,1:T(8,128)S(1)}, u32[]{:S(2)}, u32[]{:S(2)}) collective-permute-start(f32[3,1,128,128]{3,2,0,1:T(8,128)S(1)} %get-tuple-element.911), channel_id=1, source_target_pairs={{0,16},{16,32},{32,48},{48,64},{64,80},{80,96},{96,112},{112,128},... | collective-permute-start | bytes 589832 | tf_op jit(solution)/shard_map/while/body/eval_jaxpr/ppermute | solution.py:16
  143.7 9.1 collective-permute-start
  152.8 9.4 collective-permute-start
  162.2 9.7 collective-permute-start
  171.8 10.2 collective-permute-start
  182.0 11.7 collective-permute-start
  193.8 11.9 collective-permute-start
  205.6 10.6 collective-permute-start
  216.2 8.9 collective-permute-start
  225.1 9.1 collective-permute-start
  234.2 9.4 collective-permute-start
  243.6 9.7 collective-permute-start
  253.3 492.5 %collective-permute-start = (f32[3,1,128,128]{3,2,0,1:T(8,128)S(1)}, f32[3,1,128,128]{3,2,0,1:T(8,128)S(1)}, u32[]{:S(2)}, u32[]{:S(2)}) collective-permute-start(f32[3,1,128,128]{3,2,0,1:T(8,128)S(1)} %get-tuple-element.911), channel_id=1, source_target_pairs={{0,16},{16,32},{32,48},{48,64},{64,80},{80,96},{96,112},{112,128},... | collective-permute-start | bytes 589832 | tf_op jit(solution)/shard_map/while/body/eval_jaxpr/ppermute | solution.py:16
  826.2 9.0 collective-permute-start.1
  835.3 8.2 collective-permute-start.1
  843.5 7.6 collective-permute-start.1
  851.1 7.6 collective-permute-start.1
  858.6 7.8 collective-permute-start.1
  866.5 9.0 collective-permute-start.1
  875.5 9.2 collective-permute-start.1
  884.6 8.4 collective-permute-start.1
  900.6 9.3 collective-permute-start.1
  909.9 10.6 collective-permute-start.1
  920.5 9.0 collective-permute-start.1
  929.5 9.0 collective-permute-start.1
  938.5 9.4 collective-permute-start.1
  947.9 9.7 collective-permute-start.1
  957.6 284.8 %collective-permute-start.1 = (f32[3,1,128,128]{3,2,0,1:T(8,128)S(1)}, f32[3,1,128,128]{3,2,0,1:T(8,128)S(1)}, u32[]{:S(2)}, u32[]{:S(2)}) collective-permute-start(f32[3,1,128,128]{3,2,0,1:T(8,128)S(1)} %get-tuple-element.947), channel_id=1, source_target_pairs={{0,16},{16,32},{32,48},{48,64},{64,80},{80,96},{96,112},{112,128},... | collective-permute-start | bytes 589832 | tf_op jit(solution)/shard_map/while/body/eval_jaxpr/ppermute | solution.py:16
  (8 other events, 228.9 us)
